TPU v7x, 32 devices: a whole 2x2x4 slice. The times are simulated.
32 devices in a mesh: dom: 8 (over z, x), feat: 4 (over y, core).
Axes of the slice: x: 2, y: 2, z: 4, core: 2. Of those that a mesh axis runs over, the one named last changes fastest.
Arguments:
- node_feats: bfloat16 [16384, 512], P('dom', 'feat'), may hold values from -6 to 6
- edge_tiles: bfloat16 [848, 128, 128], P('dom'), may hold values from -0.14941406 to 0.14941406
- tile_dst: int32 [848], P('dom'), may hold values from 0 to 15, as said below
- tile_src: int32 [848], P('dom'), may hold values from 0 to 25, as said below
- hub_ids: int32 [256], P('dom'), may hold values from 0 to 2047, as said below
- send_rows: int32 [8, 8, 128], P('dom'), may hold values from 0 to 2047
- send_count: int32 [8, 8], P('dom'), may hold values from 32 to 128, as said below
- w_self: bfloat16 [512, 512], P(None, 'feat'), may hold values from -0.25 to 0.25
- w_neigh: bfloat16 [512, 512], P(None, 'feat'), may hold values from -0.25 to 0.25
- out_bias: float32 [512], P('feat'), may hold values from -3 to 3
- grad_out: bfloat16 [16384, 512], P('dom', 'feat'), may hold values from -6 to 6
Outputs:
- output: bfloat16 [16384, 512], P('dom', 'feat')
- grad_feats: float32 [16384, 512], P('dom', 'feat')
- grad_self: float32 [512, 512], P(None, 'feat')
- grad_neigh: float32 [512, 512], P(None, 'feat')
- grad_bias: float32 [512], P('feat')
Inputs may be any that keep to these rules, and one draw needn't show every extreme that they name: `tile_dst`: every one of the 16 blocks of a partition receives at least 5 of its tiles. `tile_src`: source blocks of a partition: its own rows, then all hub rows, then received rows in order of sender; every block is read by at least one tile of every partition. `hub_ids`: distinct within each partition. `send_count`: every partition sends exactly 128 rows to at least one partition, and some partition receives exactly 128 rows from every partition.
All inputs are finite; a program needn't handle non-finite values.
Results may differ from a plain program's by a relative error of at most 0.0055.
Values may be sent and summed in bfloat16 or wider, within the bound.
No kernel may reach another device: no remote copies, remote signals or barrier semaphores. Data moves between devices by JAX's collectives and lax.ppermute only.
A program may use at most 128 MiB of HBM per device.

v0:
```python
import jax
import jax.numpy as jnp
from jax import lax
from jax.sharding import PartitionSpec as P


def body(
    node_feats,
    edge_tiles,
    tile_dst,
    tile_src,
    hub_ids,
    send_rows,
    send_count,
    w_self,
    w_neigh,
    out_bias,
    grad_out,
):
    own_count, width = node_feats.shape
    tile_size = edge_tiles.shape[1]
    peer_count, capacity = (send_rows.shape[1], send_rows.shape[2])
    hub_local = node_feats[hub_ids]
    hub_table = lax.all_gather(hub_local, "dom", axis=0, tiled=True)
    listed = send_rows[0]
    filled = jnp.arange(capacity, dtype=jnp.int32)[None, :] < send_count[0][:, None]
    outgoing = jnp.where(filled[:, :, None], node_feats[listed], jnp.zeros((), node_feats.dtype))
    incoming = lax.all_to_all(outgoing, "dom", split_axis=0, concat_axis=0, tiled=True)
    source = jnp.concatenate(
        [node_feats, hub_table, incoming.reshape(peer_count * capacity, width)], axis=0
    )
    source_blocks = source.shape[0] // tile_size
    row_blocks = own_count // tile_size
    blocks = source.reshape(source_blocks, tile_size, width)
    products = jnp.einsum(
        "tij,tjf->tif", edge_tiles, blocks[tile_src], preferred_element_type=jnp.float32
    )
    summed = jax.ops.segment_sum(products, tile_dst, row_blocks)
    aggregated = summed.reshape(own_count, width).astype(jnp.bfloat16)
    whole_feats, whole_agg = (
        lax.all_gather(node_feats, "feat", axis=1, tiled=True),
        lax.all_gather(aggregated, "feat", axis=1, tiled=True),
    )
    pre_act = (
        jnp.dot(whole_feats, w_self, preferred_element_type=jnp.float32)
        + jnp.dot(whole_agg, w_neigh, preferred_element_type=jnp.float32)
        + out_bias
    )
    gate_sig = jax.nn.sigmoid(pre_act)
    output = (pre_act * gate_sig).astype(jnp.bfloat16)
    grad_pre = (
        grad_out.astype(jnp.float32) * gate_sig * (1.0 + pre_act * (1.0 - gate_sig))
    ).astype(jnp.bfloat16)
    contract_rows = (((0,), (0,)), ((), ()))
    grad_self = lax.dot_general(
        whole_feats, grad_pre, contract_rows, preferred_element_type=jnp.float32
    )
    grad_neigh = lax.dot_general(
        whole_agg, grad_pre, contract_rows, preferred_element_type=jnp.float32
    )
    grad_bias = jnp.sum(grad_pre.astype(jnp.float32), axis=0)
    grad_self, grad_neigh, grad_bias = lax.psum((grad_self, grad_neigh, grad_bias), "dom")
    contract_last = (((1,), (1,)), ((), ()))
    first = lax.dot_general(w_self, grad_pre, contract_last, preferred_element_type=jnp.float32)
    second = lax.dot_general(w_neigh, grad_pre, contract_last, preferred_element_type=jnp.float32)
    shares = lax.psum_scatter(
        jnp.concatenate([first, second], axis=1), "feat", scatter_dimension=0, tiled=True
    )
    direct = shares[:, :own_count].T
    back_agg = shares[:, own_count:].T.astype(jnp.bfloat16)
    back_blocks = back_agg.reshape(row_blocks, tile_size, width)[tile_dst]
    spread = jnp.einsum("tji,tjf->tif", edge_tiles, back_blocks, preferred_element_type=jnp.float32)
    back_source = jax.ops.segment_sum(spread, tile_src, source_blocks).reshape(-1, width)
    hub_total = hub_table.shape[0]
    hub_part = back_source[own_count : own_count + hub_total]
    recv_part = back_source[own_count + hub_total :].reshape(peer_count, capacity, width)
    hub_back = lax.psum_scatter(hub_part, "dom", scatter_dimension=0, tiled=True)
    sent_back = lax.all_to_all(
        recv_part.astype(jnp.bfloat16), "dom", split_axis=0, concat_axis=0, tiled=True
    ).astype(recv_part.dtype)
    returned = jnp.where(filled[:, :, None], sent_back, jnp.zeros((), jnp.float32))
    grad_feats = direct + back_source[:own_count]
    grad_feats = grad_feats.at[hub_ids].add(hub_back)
    grad_feats = grad_feats.at[listed.reshape(-1)].add(
        returned.reshape(peer_count * capacity, width)
    )
    return (output, grad_feats, grad_self, grad_neigh, grad_bias)


def solution(mesh):
    in_specs = (
        P("dom", "feat"),
        P("dom", None, None),
        P("dom"),
        P("dom"),
        P("dom"),
        P("dom", None, None),
        P("dom", None),
        P(None, "feat"),
        P(None, "feat"),
        P("feat"),
        P("dom", "feat"),
    )
    out_specs = (P("dom", "feat"), P("dom", "feat"), P(None, "feat"), P(None, "feat"), P("feat"))
    return jax.shard_map(body, mesh=mesh, in_specs=in_specs, out_specs=out_specs, check_vma=False)
```

profile of v0, /device:TPU:0, one launch (start us, length us, event | category | flops | bytes accessed | tf_op | source)
XLA Modules:
  0.0 419.5 jit_solution(15320924251841132812)
XLA Ops:
  7.2 0.0 copy-start
  7.2 0.0 copy-start.8
  7.2 0.0 all-gather.4.cloned.1.call-start
  7.2 0.7 all-gather.4.cloned.1.call-update
  7.9 0.8 fusion.3
  8.8 5.2 %gather_fusion.1 = bf16[1024,128]{1,0:T(8,128)(2,1)} fusion(bf16[2048,128]{1,0:T(8,128)(2,1)} %param.11, s32[1024]{0:T(1024)S(1)} %fusion.3), kind=kCustom, calls=%fused_computation.1 | custom fusion | bytes 528384 | tf_op jit(solution)/shard_map/gather | solution.py:27
  14.0 0.7 iota_compare_fusion
  14.7 1.9 broadcast_select_fusion
  16.5 7.3 %all-to-all-start = ((bf16[8,128,128]{2,1,0:T(8,128)(2,1)}), bf16[8,128,128]{2,1,0:T(8,128)(2,1)}, u32[]{:S(2)}, u32[]{:S(2)}) async-start(bf16[8,128,128]{2,1,0:T(8,128)(2,1)} %broadcast_select_fusion), calls=%async_computation | async-start | bytes 524288 | tf_op jit(solution)/shard_map/all_to_all | solution.py:28
  23.8 0.0 all-gather.6.cloned.1.call-start
  23.8 0.0 copy-done.8
  23.9 1.7 gather_fusion
  25.6 31.1 %all-gather = bf16[256,128]{1,0:T(8,128)(2,1)S(1)} all-gather(bf16[32,128]{1,0:T(8,128)(2,1)S(1)} %gather_fusion), channel_id=2, replica_groups=mesh['dom'=8,'feat'=4] {'dom'}, dimensions={0}, use_global_device_ids=true | all-gather | bytes 73728 | tf_op jit(solution)/shard_map/all_gather | solution.py:24
  56.7 0.7 compare_select_fusion.3
  57.4 0.0 all-to-all-done
  57.4 2.1 pad_maximum_fusion.1
  59.5 4.0 gather_fusion.2
  63.5 0.0 copy-done
  63.5 7.4 %convolution_bitcast_fusion.3 = f32[106,128,128]{1,2,0:T(8,128)} fusion(bf16[106,128,128]{2,1,0:T(8,128)(2,1)} %gather_fusion.2, bf16[106,128,128]{2,1,0:T(8,128)(2,1)S(1)} %copy-done), kind=kOutput, calls=%fused_computation.12 | convolution fusion | flops 444596224 | bytes 13893632 | tf_op jit(solution)/shard_map/tij,tjf->tif/dot_general | solution.py:35
  70.9 8.3 %copy.20 = f32[106,128,128]{2,1,0:T(8,128)} copy(f32[106,128,128]{1,2,0:T(8,128)} %convolution_bitcast_fusion.3) | data formatting | bytes 13893632 | tf_op jit(solution)/shard_map/tij,tjf->tif/dot_general | solution.py:35
  79.2 1.1 broadcast_in_dim.50
  80.3 0.0 copy-done.6
  80.3 22.4 %scatter_fusion = f32[16,128,128]{2,1,0:T(8,128)} fusion(f32[16,128,128]{2,1,0:T(8,128)} %broadcast_in_dim.50, s32[106]{0:T(128)S(1)} %copy-done.6, f32[106,128,128]{2,1,0:T(8,128)} %copy.20), kind=kCustom, calls=%fused_computation.4 | custom fusion | flops 1736704 | bytes 20840872 | tf_op jit(solution)/shard_map/scatter-add | solution.py:38
  102.7 2.1 convert_element_type.26
  104.8 0.0 all-gather.6.cloned.1.call-update
  104.8 0.0 all-reduce.3.cloned.1.call-start
  104.9 0.0 all-gather.4.cloned.1.call-done
  104.9 3.3 fusion.4
  108.2 20.4 %all-gather.6.cloned.1.call-done = bf16[2048,512]{1,0:T(8,128)(2,1)} async-done(((bf16[2048,128]{1,0:T(8,128)(2,1)}), bf16[2048,512]{1,0:T(8,128)(2,1)}) %all-gather.6.cloned.1.call-update) | async-done | bytes 2097168 | tf_op jit(solution)/shard_map/all_gather | solution.py:42
  128.6 0.0 copy-done.9
  128.6 3.7 convert_reduce_fusion
  132.3 0.0 copy-done.4
  132.3 2.7 convolution_bitcast_fusion
  135.0 2.8 convolution_bitcast_fusion.1
  137.7 1.4 fusion.5
  139.2 1.2 convolution_bitcast_fusion.4
  140.4 0.0 all-reduce.3.cloned.1.call-update
  140.4 0.0 reduce-scatter.3.cloned.1.call-start
  140.4 7.7 %pad_maximum_fusion = f32[512,4096]{0,1:T(8,128)} fusion(f32[512,2048]{0,1:T(8,128)} %convolution_bitcast_fusion, f32[512,2048]{0,1:T(8,128)} %convolution_bitcast_fusion.1), kind=kLoop, calls=%fused_computation.8 | loop fusion | flops 2097152 | bytes 16777216 | tf_op jit(solution)/shard_map/concatenate | solution.py:67
  148.1 0.0 reduce-scatter.3.cloned.1.call-update
  148.2 0.0 reduce-scatter.5.cloned.1.call-start
  148.2 0.6 copy-done.5
  148.8 22.0 %psum.23 = f32[128]{0:T(128)} all-reduce(f32[128]{0:T(128)S(1)} %get-tuple-element.17), channel_id=1, replica_groups=mesh['dom'=8,'feat'=4] {'dom'}, use_global_device_ids=true, to_apply=%region_9.10 | all-reduce | flops 128 | bytes 1024 | tf_op jit(solution)/shard_map/psum | solution.py:62
  170.9 42.4 %all-reduce.3.cloned.1.call-done = (f32[512,128]{0,1:T(8,128)}, f32[512,128]{1,0:T(8,128)}) async-done(((f32[512,128]{0,1:T(8,128)}, f32[512,128]{1,0:T(8,128)}), (f32[512,128]{0,1:T(8,128)}, f32[512,128]{1,0:T(8,128)})) %all-reduce.3.cloned.1.call-update) | async-done | bytes 524304 | tf_op jit(solution)/shard_map/psum | solution.py:62
  213.2 1.8 copy.23
  215.0 71.8 %reduce-scatter.3.cloned.1.call-done = f32[128,4096]{0,1:T(8,128)} async-done(((f32[512,4096]{0,1:T(8,128)}), f32[128,4096]{0,1:T(8,128)}) %reduce-scatter.3.cloned.1.call-update) | async-done | bytes 2097168 | tf_op jit(solution)/shard_map/reduce_scatter | solution.py:66
  286.8 2.1 slice.49
  288.9 3.8 gather_fusion.3
  292.7 6.2 %convolution_bitcast_fusion.2 = f32[106,128,128]{1,2,0:T(8,128)} fusion(bf16[106,128,128]{2,1,0:T(8,128)(2,1)} %gather_fusion.3, bf16[106,128,128]{2,1,0:T(8,128)(2,1)S(1)} %copy-done), kind=kOutput, calls=%fused_computation.11 | convolution fusion | flops 444596224 | bytes 13893632 | tf_op jit(solution)/shard_map/tji,tjf->tif/dot_general | solution.py:72
  298.9 8.3 %copy.22 = f32[106,128,128]{2,1,0:T(8,128)} copy(f32[106,128,128]{1,2,0:T(8,128)} %convolution_bitcast_fusion.2) | data formatting | bytes 13893632 | tf_op jit(solution)/shard_map/tji,tjf->tif/dot_general | solution.py:72
  307.2 1.4 broadcast_in_dim.56
  308.6 22.7 %scatter_fusion.1 = f32[26,128,128]{2,1,0:T(8,128)} fusion(f32[26,128,128]{2,1,0:T(8,128)} %broadcast_in_dim.56, s32[106]{0:T(128)S(1)} %copy-done.7, f32[106,128,128]{2,1,0:T(8,128)} %copy.22), kind=kCustom, calls=%fused_computation.5 | custom fusion | flops 1736704 | bytes 20840872 | tf_op jit(solution)/shard_map/scatter-add | solution.py:73
  331.4 1.6 slice.42
  333.0 1.8 slice.50
  334.8 2.4 slice.41
  337.1 0.0 reduce-scatter.5.cloned.1.call-update
  337.2 5.6 %all-to-all-start.1 = ((bf16[8,128,128]{2,1,0:T(8,128)(2,1)}), bf16[8,128,128]{2,1,0:T(8,128)(2,1)}, u32[]{:S(2)}, u32[]{:S(2)}) async-start(bf16[8,128,128]{2,1,0:T(8,128)(2,1)} %slice.50), calls=%async_computation.3 | async-start | bytes 524288 | tf_op jit(solution)/shard_map/all_to_all | solution.py:78
  342.7 2.6 fusion.1
  345.3 53.0 %reduce-scatter.5.cloned.1.call-done = f32[32,128]{1,0:T(8,128)} async-done(((f32[256,128]{1,0:T(8,128)}), f32[32,128]{1,0:T(8,128)}) %reduce-scatter.5.cloned.1.call-update) | async-done | bytes 16400 | tf_op jit(solution)/shard_map/reduce_scatter | solution.py:77
  398.3 3.1 scatter_fusion.2
  401.4 0.0 all-to-all-done.1
  401.4 1.9 convert_select_fusion
  403.3 8.0 %scatter_fusion.3 = f32[2048,128]{1,0:T(8,128)} fusion(f32[2048,128]{1,0:T(8,128)} %scatter_fusion.2, s32[1024]{0:T(1024)S(1)} %bitcast.56, f32[1024,128]{1,0:T(8,128)} %bitcast.53), kind=kCustom, calls=%fused_computation.7 | custom fusion | flops 131072 | bytes 1576960 | tf_op jit(solution)/shard_map/scatter-add | solution.py:84
  411.3 1.7 copy.32
  (18 shorter events, 0.1 us)
Async XLA Ops:
  7.2 56.3 %copy-start = (bf16[106,128,128]{2,1,0:T(8,128)(2,1)S(1)}, bf16[106,128,128]{2,1,0:T(8,128)(2,1)}, u32[]{:S(2)}) copy-start(bf16[106,128,128]{2,1,0:T(8,128)(2,1)} %param.12) | copy-start | bytes 10420228
  7.2 16.7 %copy-start.8 = (s32[32]{0:T(128)S(1)}, s32[32]{0:T(128)}, u32[]{:S(2)}) copy-start(s32[32]{0:T(128)} %param.15) | copy-start | bytes 388
  7.2 97.7 %all-gather.4.cloned.1.call-start = ((), (), s32[]{:S(2)}) async-start(), calls=%async_computation.4 | async-start | bytes 2621440 | tf_op jit(solution)/shard_map/all_gather | solution.py:41
  16.5 40.8 %all-to-all-start = ((bf16[8,128,128]{2,1,0:T(8,128)(2,1)}), bf16[8,128,128]{2,1,0:T(8,128)(2,1)}, u32[]{:S(2)}, u32[]{:S(2)}) async-start(bf16[8,128,128]{2,1,0:T(8,128)(2,1)} %broadcast_select_fusion), calls=%async_computation | async-start | bytes 524288 | tf_op jit(solution)/shard_map/all_to_all | solution.py:28
  23.8 104.8 %all-gather.6.cloned.1.call-start = ((), (), s32[]{:S(2)}) async-start(), calls=%async_computation.5 | async-start | bytes 2621440 | tf_op jit(solution)/shard_map/all_gather | solution.py:42
  70.9 9.4 %copy-start.6 = (s32[106]{0:T(128)S(1)}, s32[106]{0:T(128)}, u32[]{:S(2)}) copy-start(s32[106]{0:T(128)} %param.13) | copy-start | bytes 1276
  102.7 25.9 %copy-start.9 = (f32[128]{0:T(128)S(1)}, f32[128]{0:T(128)}, u32[]{:S(2)}) copy-start(f32[128]{0:T(128)} %param.20) | copy-start | bytes 1540
  104.8 108.4 %all-reduce.3.cloned.1.call-start = ((), (), s32[]{:S(2)}) async-start(), calls=%async_computation.8 | async-start | bytes 1048576 | tf_op jit(solution)/shard_map/psum | solution.py:62
  128.6 3.7 copy-start.4
  132.3 2.7 copy-start.3
  135.0 2.8 copy-start.2
  135.0 4.2 %copy-start.1 = (bf16[2048,512]{1,0:T(8,128)(2,1)S(1)}, bf16[2048,512]{1,0:T(8,128)(2,1)}, u32[]{:S(2)}) copy-start(bf16[2048,512]{1,0:T(8,128)(2,1)} %all-gather.4.cloned.1.call-done) | copy-start | bytes 6291460
  140.4 146.4 %reduce-scatter.3.cloned.1.call-start = ((), (), s32[]{:S(2)}) async-start(), calls=%async_computation.6 | async-start | bytes 10485760 | tf_op jit(solution)/shard_map/reduce_scatter | solution.py:66
  148.1 0.7 copy-start.5
  148.2 250.1 %reduce-scatter.5.cloned.1.call-start = ((), (), s32[]{:S(2)}) async-start(), calls=%async_computation.7 | async-start | bytes 147456 | tf_op jit(solution)/shard_map/reduce_scatter | solution.py:77
  298.9 9.7 %copy-start.7 = (s32[106]{0:T(128)S(1)}, s32[106]{0:T(128)}, u32[]{:S(2)}) copy-start(s32[106]{0:T(128)} %param.14) | copy-start | bytes 1276
  337.2 64.2 %all-to-all-start.1 = ((bf16[8,128,128]{2,1,0:T(8,128)(2,1)}), bf16[8,128,128]{2,1,0:T(8,128)(2,1)}, u32[]{:S(2)}, u32[]{:S(2)}) async-start(bf16[8,128,128]{2,1,0:T(8,128)(2,1)} %slice.50), calls=%async_computation.3 | async-start | bytes 524288 | tf_op jit(solution)/shard_map/all_to_all | solution.py:78
Sparse Core Ops, SparseCore 0:
  9.6 25.5 all-gather.3
  105.0 23.6 all-gather.5
  140.5 72.6 all-reduce.2
  215.8 70.9 reduce-scatter.2
  337.3 60.9 reduce-scatter.4
where the time goes:
time: 421 us; the launch traced here: 420 us
  waiting for transfers between devices  188 us (45%)
  other arithmetic  76.7 us (18%)
  blocking collectives  53.2 us (13%)
  local copies, waits for them, and re-layouts  45.8 us (11%)
  matrix products  28.6 us (7%)
  between operations  13.9 us (3%)
  starting transfers between devices  13 us (3%)
    reduce_scatter x1, waiting for transfers between devices, body(): lax.psum_scatter(jnp.concatenate([first, second], axis=1), 'feat', scatte...  71.8 us
    reduce_scatter x1, waiting for transfers between devices, body(): lax.psum_scatter(hub_part, 'dom', scatter_dimension=0, tiled=True)  53 us
    psum x1, waiting for transfers between devices, body(): lax.psum((grad_self, grad_neigh, grad_bias), 'dom')  42.4 us
    all_gather x1, blocking collectives, body(): hub_table = lax.all_gather(hub_local, 'dom', axis=0, tiled=True)  31.1 us
    scatter-add x1, other arithmetic, body(): jax.ops.segment_sum(spread, tile_src, source_blocks).reshape(-1, width)  22.7 us
    scatter-add x1, other arithmetic, body(): summed = jax.ops.segment_sum(products, tile_dst, row_blocks)  22.4 us
    psum x1, blocking collectives, body(): lax.psum((grad_self, grad_neigh, grad_bias), 'dom')  22 us
    all_gather x1, waiting for transfers between devices, body(): lax.all_gather(aggregated, 'feat', axis=1, tiled=True)  20.4 us
  transfers between devices with their start and end apart: 7, of which 4 were waited for; matrix products, arithmetic and copies ran while one was open for 18% of the time, Pallas kernels for 0%

commit v1 on v0

--- a/solution.py
+++ b/solution.py
@@ -2,6 +2,18 @@
 import jax.numpy as jnp
 from jax import lax
 from jax.sharding import PartitionSpec as P
+
+
+def collect(x, axis, dim):
+    ways, here = (lax.axis_size(axis), lax.axis_index(axis))
+    grown, reach = (x, 1)
+    while reach < ways:
+        theirs = lax.ppermute(grown, axis, [(d, d ^ reach) for d in range(ways)])
+        mine_first = jnp.concatenate([grown, theirs], axis=dim)
+        theirs_first = jnp.concatenate([theirs, grown], axis=dim)
+        grown = jnp.where(here & reach == 0, mine_first, theirs_first)
+        reach = 2 * reach
+    return grown
 
 
 def body(
@@ -21,7 +33,7 @@
     tile_size = edge_tiles.shape[1]
     peer_count, capacity = (send_rows.shape[1], send_rows.shape[2])
     hub_local = node_feats[hub_ids]
-    hub_table = lax.all_gather(hub_local, "dom", axis=0, tiled=True)
+    hub_table = collect(hub_local, "dom", 0)
     listed = send_rows[0]
     filled = jnp.arange(capacity, dtype=jnp.int32)[None, :] < send_count[0][:, None]
     outgoing = jnp.where(filled[:, :, None], node_feats[listed], jnp.zeros((), node_feats.dtype))

time: 421 us -> 403 us (0.957)
  blocking collectives: 53.2 us -> 22 us
  starting transfers between devices: 13 us -> 18.8 us
  waiting for transfers between devices: 188 us -> 193 us
    all_gather x1 -> x0, blocking collectives: 31.1 us -> none  [body(): hub_table = lax.all_gather(hub_local, 'dom', axis=0, tiled=True)]
    ppermute x0 -> x3, starting transfers between devices: none -> 8.14 us  [collect(): theirs = lax.ppermute(grown, axis, [(d, d ^ reach) for d in range(ways)])]
    ppermute x0 -> x3, waiting for transfers between devices: none -> 4.68 us  [collect(): theirs = lax.ppermute(grown, axis, [(d, d ^ reach) for d in range(ways)])]
  transfers between devices with their start and end apart: 7 -> 10, of which waited for: 4 -> 6; matrix products, arithmetic and copies ran while one was open for 18% -> 20% of each run, Pallas kernels for 0% -> 0%
where the time goes in v1:
time: 403 us; the launch traced here: 401 us
  waiting for transfers between devices  193 us (48%)
  other arithmetic  78.9 us (20%)
  local copies, waits for them, and re-layouts  45.7 us (11%)
  matrix products  28.6 us (7%)
  blocking collectives  22 us (5%)
  starting transfers between devices  18.8 us (5%)
  between operations  13.9 us (3%)
    reduce_scatter x1, waiting for transfers between devices, body(): lax.psum_scatter(jnp.concatenate([first, second], axis=1), 'feat', scatte...  71.8 us
    reduce_scatter x1, waiting for transfers between devices, body(): lax.psum_scatter(hub_part, 'dom', scatter_dimension=0, tiled=True)  53 us
    psum x1, waiting for transfers between devices, body(): lax.psum((grad_self, grad_neigh, grad_bias), 'dom')  42.4 us
    scatter-add x1, other arithmetic, body(): jax.ops.segment_sum(spread, tile_src, source_blocks).reshape(-1, width)  22.9 us
    scatter-add x1, other arithmetic, body(): summed = jax.ops.segment_sum(products, tile_dst, row_blocks)  22.4 us
    psum x1, blocking collectives, body(): lax.psum((grad_self, grad_neigh, grad_bias), 'dom')  22 us
    all_gather x1, waiting for transfers between devices, body(): lax.all_gather(aggregated, 'feat', axis=1, tiled=True)  20.2 us
    dot_general x1, local copies, waits for them, and re-layouts, body(): jnp.einsum('tij,tjf->tif', edge_tiles, blocks[tile_src], preferred_elemen...  8.35 us
  transfers between devices with their start and end apart: 10, of which 6 were waited for; matrix products, arithmetic and copies ran while one was open for 20% of the time, Pallas kernels for 0%

profile of v1, /device:TPU:0, one launch (start us, length us, event | category | flops | bytes accessed | tf_op | source)
XLA Modules:
  0.0 400.8 jit_solution(10952055561778916014)
XLA Ops:
  7.2 0.0 copy-start
  7.2 0.0 all-gather.3.cloned.1.call-start
  7.2 0.7 all-gather.3.cloned.1.call-update
  7.9 0.8 compare_select_fusion.4
  8.7 1.7 gather_fusion
  10.4 3.0 collective-permute-start
  13.4 0.7 fusion.3
  14.1 5.2 %gather_fusion.1 = bf16[1024,128]{1,0:T(8,128)(2,1)} fusion(bf16[2048,128]{1,0:T(8,128)(2,1)} %param.11, s32[1024]{0:T(1024)S(1)} %fusion.3), kind=kCustom, calls=%fused_computation.1 | custom fusion | bytes 528384 | tf_op jit(solution)/shard_map/gather | solution.py:39
  19.3 0.7 iota_compare_fusion
  20.0 1.9 broadcast_select_fusion
  21.9 4.9 %all-to-all-start = ((bf16[8,128,128]{2,1,0:T(8,128)(2,1)}), bf16[8,128,128]{2,1,0:T(8,128)(2,1)}, u32[]{:S(2)}, u32[]{:S(2)}) async-start(bf16[8,128,128]{2,1,0:T(8,128)(2,1)} %broadcast_select_fusion), calls=%async_computation | async-start | bytes 524288 | tf_op jit(solution)/shard_map/all_to_all | solution.py:40
  26.8 0.0 all-gather.5.cloned.1.call-start
  26.9 2.0 collective-permute-start.1
  28.9 0.5 compare_select_fusion.3
  29.4 3.3 collective-permute-done.1
  32.7 0.0 copy-start.5
  32.8 3.1 collective-permute-start.2
  35.9 0.7 pad_clamp_fusion.1
  36.5 1.3 collective-permute-done.2
  37.9 0.9 maximum_select_fusion
  38.7 2.1 pad_maximum_fusion.1
  40.8 4.0 %gather_fusion.2 = bf16[106,128,128]{2,1,0:T(8,128)(2,1)} fusion(bf16[26,128,128]{2,1,0:T(8,128)(2,1)} %bitcast.51, s32[1024]{0:T(1024)S(1)} %pad_clamp_fusion.1), kind=kCustom, calls=%fused_computation.2 | custom fusion | bytes 6947240 | tf_op jit(solution)/shard_map/gather | solution.py:48
  44.8 7.4 %convolution_bitcast_fusion.3 = f32[106,128,128]{1,2,0:T(8,128)} fusion(bf16[106,128,128]{2,1,0:T(8,128)(2,1)} %gather_fusion.2, bf16[106,128,128]{2,1,0:T(8,128)(2,1)S(1)} %copy-done), kind=kOutput, calls=%fused_computation.12 | convolution fusion | flops 444596224 | bytes 13893632 | tf_op jit(solution)/shard_map/tij,tjf->tif/dot_general | solution.py:47
  52.3 8.4 %copy.20 = f32[106,128,128]{2,1,0:T(8,128)} copy(f32[106,128,128]{1,2,0:T(8,128)} %convolution_bitcast_fusion.3) | data formatting | bytes 13893632 | tf_op jit(solution)/shard_map/tij,tjf->tif/dot_general | solution.py:47
  60.6 1.1 broadcast_in_dim.50
  61.7 22.4 %scatter_fusion = f32[16,128,128]{2,1,0:T(8,128)} fusion(f32[16,128,128]{2,1,0:T(8,128)} %broadcast_in_dim.50, s32[106]{0:T(128)S(1)} %copy-done.7, f32[106,128,128]{2,1,0:T(8,128)} %copy.20), kind=kCustom, calls=%fused_computation.4 | custom fusion | flops 1736704 | bytes 20840872 | tf_op jit(solution)/shard_map/scatter-add | solution.py:50
  84.1 2.1 convert_element_type.26
  86.2 0.0 all-gather.5.cloned.1.call-update
  86.2 0.0 all-reduce.3.cloned.1.call-start
  86.3 0.0 all-gather.3.cloned.1.call-done
  86.3 3.3 fusion.4
  89.6 20.2 %all-gather.5.cloned.1.call-done = bf16[2048,512]{1,0:T(8,128)(2,1)} async-done(((bf16[2048,128]{1,0:T(8,128)(2,1)}), bf16[2048,512]{1,0:T(8,128)(2,1)}) %all-gather.5.cloned.1.call-update) | async-done | bytes 2097168 | tf_op jit(solution)/shard_map/all_gather | solution.py:54
  109.8 3.7 convert_reduce_fusion
  113.5 2.7 convolution_bitcast_fusion
  116.1 2.8 convolution_bitcast_fusion.1
  118.9 1.4 fusion.5
  120.4 1.2 convolution_bitcast_fusion.4
  121.5 0.0 all-reduce.3.cloned.1.call-update
  121.5 0.0 reduce-scatter.3.cloned.1.call-start
  121.6 7.7 %pad_maximum_fusion = f32[512,4096]{0,1:T(8,128)} fusion(f32[512,2048]{0,1:T(8,128)} %convolution_bitcast_fusion, f32[512,2048]{0,1:T(8,128)} %convolution_bitcast_fusion.1), kind=kLoop, calls=%fused_computation.8 | loop fusion | flops 2097152 | bytes 16777216 | tf_op jit(solution)/shard_map/concatenate | solution.py:79
  129.3 0.0 reduce-scatter.3.cloned.1.call-update
  129.3 0.0 reduce-scatter.5.cloned.1.call-start
  129.4 0.6 copy-done.6
  130.0 22.0 %psum.23 = f32[128]{0:T(128)} all-reduce(f32[128]{0:T(128)S(1)} %get-tuple-element.17), channel_id=1, replica_groups=mesh['dom'=8,'feat'=4] {'dom'}, use_global_device_ids=true, to_apply=%region_9.10 | all-reduce | flops 128 | bytes 1024 | tf_op jit(solution)/shard_map/psum | solution.py:74
  152.0 42.4 %all-reduce.3.cloned.1.call-done = (f32[512,128]{0,1:T(8,128)}, f32[512,128]{1,0:T(8,128)}) async-done(((f32[512,128]{0,1:T(8,128)}, f32[512,128]{1,0:T(8,128)}), (f32[512,128]{0,1:T(8,128)}, f32[512,128]{1,0:T(8,128)})) %all-reduce.3.cloned.1.call-update) | async-done | bytes 524304 | tf_op jit(solution)/shard_map/psum | solution.py:74
  194.4 1.8 copy.23
  196.2 71.8 %reduce-scatter.3.cloned.1.call-done = f32[128,4096]{0,1:T(8,128)} async-done(((f32[512,4096]{0,1:T(8,128)}), f32[128,4096]{0,1:T(8,128)}) %reduce-scatter.3.cloned.1.call-update) | async-done | bytes 2097168 | tf_op jit(solution)/shard_map/reduce_scatter | solution.py:78
  268.0 2.1 slice.49
  270.1 3.8 gather_fusion.3
  273.9 6.2 %convolution_bitcast_fusion.2 = f32[106,128,128]{1,2,0:T(8,128)} fusion(bf16[106,128,128]{2,1,0:T(8,128)(2,1)} %gather_fusion.3, bf16[106,128,128]{2,1,0:T(8,128)(2,1)S(1)} %copy-done), kind=kOutput, calls=%fused_computation.11 | convolution fusion | flops 444596224 | bytes 13893632 | tf_op jit(solution)/shard_map/tji,tjf->tif/dot_general | solution.py:84
  280.1 8.3 %copy.22 = f32[106,128,128]{2,1,0:T(8,128)} copy(f32[106,128,128]{1,2,0:T(8,128)} %convolution_bitcast_fusion.2) | data formatting | bytes 13893632 | tf_op jit(solution)/shard_map/tji,tjf->tif/dot_general | solution.py:84
  288.4 1.4 broadcast_in_dim.56
  289.8 22.9 %scatter_fusion.1 = f32[26,128,128]{2,1,0:T(8,128)} fusion(f32[26,128,128]{2,1,0:T(8,128)} %broadcast_in_dim.56, s32[106]{0:T(128)S(1)} %copy-done.8, f32[106,128,128]{2,1,0:T(8,128)} %copy.22), kind=kCustom, calls=%fused_computation.5 | custom fusion | flops 1736704 | bytes 20840872 | tf_op jit(solution)/shard_map/scatter-add | solution.py:85
  312.7 2.4 slice.41
  315.1 1.6 slice.42
  316.7 1.8 slice.50
  318.4 0.0 reduce-scatter.5.cloned.1.call-update
  318.5 5.6 %all-to-all-start.1 = ((bf16[8,128,128]{2,1,0:T(8,128)(2,1)}), bf16[8,128,128]{2,1,0:T(8,128)(2,1)}, u32[]{:S(2)}, u32[]{:S(2)}) async-start(bf16[8,128,128]{2,1,0:T(8,128)(2,1)} %slice.50), calls=%async_computation.3 | async-start | bytes 524288 | tf_op jit(solution)/shard_map/all_to_all | solution.py:90
  324.0 2.6 fusion.1
  326.6 53.0 %reduce-scatter.5.cloned.1.call-done = f32[32,128]{1,0:T(8,128)} async-done(((f32[256,128]{1,0:T(8,128)}), f32[32,128]{1,0:T(8,128)}) %reduce-scatter.5.cloned.1.call-update) | async-done | bytes 16400 | tf_op jit(solution)/shard_map/reduce_scatter | solution.py:89
  379.6 3.1 scatter_fusion.2
  382.7 2.0 convert_select_fusion
  384.6 8.0 %scatter_fusion.3 = f32[2048,128]{1,0:T(8,128)} fusion(f32[2048,128]{1,0:T(8,128)} %scatter_fusion.2, s32[1024]{0:T(1024)S(1)} %bitcast.56, f32[1024,128]{1,0:T(8,128)} %bitcast.53), kind=kCustom, calls=%fused_computation.7 | custom fusion | flops 131072 | bytes 1576960 | tf_op jit(solution)/shard_map/scatter-add | solution.py:96
  392.6 1.7 copy.32
  (26 shorter events, 0.1 us)
Async XLA Ops:
  7.2 37.7 %copy-start = (bf16[106,128,128]{2,1,0:T(8,128)(2,1)S(1)}, bf16[106,128,128]{2,1,0:T(8,128)(2,1)}, u32[]{:S(2)}) copy-start(bf16[106,128,128]{2,1,0:T(8,128)(2,1)} %param.12) | copy-start | bytes 10420228
  7.2 21.7 %copy-start.8 = (s32[106]{0:T(128)S(1)}, s32[106]{0:T(128)}, u32[]{:S(2)}) copy-start(s32[106]{0:T(128)} %param.14) | copy-start | bytes 1276
  7.2 79.1 %all-gather.3.cloned.1.call-start = ((), (), s32[]{:S(2)}) async-start(), calls=%async_computation.4 | async-start | bytes 2621440 | tf_op jit(solution)/shard_map/all_gather | solution.py:53
  10.4 16.4 %collective-permute-start = (bf16[32,128]{1,0:T(8,128)(2,1)S(1)}, bf16[32,128]{1,0:T(8,128)(2,1)S(1)}, u32[]{:S(2)}, u32[]{:S(2)}) collective-permute-start(bf16[32,128]{1,0:T(8,128)(2,1)S(1)} %gather_fusion), channel_id=1, source_target_pairs={{0,4},{4,0},{8,12},{12,8},{16,20},{20,16},{24,28},{28,24},{1,5},{5... | collective-permute-start | bytes 24584 | tf_op jit(solution)/shard_map/ppermute | solution.py:11
  21.9 16.8 %all-to-all-start = ((bf16[8,128,128]{2,1,0:T(8,128)(2,1)}), bf16[8,128,128]{2,1,0:T(8,128)(2,1)}, u32[]{:S(2)}, u32[]{:S(2)}) async-start(bf16[8,128,128]{2,1,0:T(8,128)(2,1)} %broadcast_select_fusion), calls=%async_computation | async-start | bytes 524288 | tf_op jit(solution)/shard_map/all_to_all | solution.py:40
  26.8 83.0 %all-gather.5.cloned.1.call-start = ((), (), s32[]{:S(2)}) async-start(), calls=%async_computation.5 | async-start | bytes 2621440 | tf_op jit(solution)/shard_map/all_gather | solution.py:54
  26.9 5.9 %collective-permute-start.1 = (bf16[64,128]{1,0:T(8,128)(2,1)S(1)}, bf16[64,128]{1,0:T(8,128)(2,1)S(1)}, u32[]{:S(2)}, u32[]{:S(2)}) collective-permute-start(bf16[64,128]{1,0:T(8,128)(2,1)S(1)} %maximum_select_fusion.2), channel_id=1, source_target_pairs={{0,8},{4,12},{8,0},{12,4},{16,24},{20,28},{24,16},{28,20},{1,9},{5... | collective-permute-start | bytes 49160 | tf_op jit(solution)/shard_map/ppermute | solution.py:11
  32.7 3.8 copy-start.5
  32.8 5.1 %collective-permute-start.2 = (bf16[128,128]{1,0:T(8,128)(2,1)S(1)}, bf16[128,128]{1,0:T(8,128)(2,1)}, u32[]{:S(2)}, u32[]{:S(2)}) collective-permute-start(bf16[128,128]{1,0:T(8,128)(2,1)S(1)} %maximum_select_fusion.1), channel_id=1, source_target_pairs={{0,16},{4,20},{8,24},{12,28},{16,0},{20,4},{24,8},{28,12},{1,17},{... | collective-permute-start | bytes 98312 | tf_op jit(solution)/shard_map/ppermute | solution.py:11
  52.3 9.4 %copy-start.7 = (s32[106]{0:T(128)S(1)}, s32[106]{0:T(128)}, u32[]{:S(2)}) copy-start(s32[106]{0:T(128)} %param.13) | copy-start | bytes 1276
  84.1 25.7 %copy-start.9 = (f32[128]{0:T(128)S(1)}, f32[128]{0:T(128)}, u32[]{:S(2)}) copy-start(f32[128]{0:T(128)} %param.20) | copy-start | bytes 1540
  86.2 108.2 %all-reduce.3.cloned.1.call-start = ((), (), s32[]{:S(2)}) async-start(), calls=%async_computation.8 | async-start | bytes 1048576 | tf_op jit(solution)/shard_map/psum | solution.py:74
  109.8 3.7 copy-start.4
  113.5 2.7 copy-start.3
  116.1 2.8 copy-start.2
  116.1 4.2 %copy-start.1 = (bf16[2048,512]{1,0:T(8,128)(2,1)S(1)}, bf16[2048,512]{1,0:T(8,128)(2,1)}, u32[]{:S(2)}) copy-start(bf16[2048,512]{1,0:T(8,128)(2,1)} %all-gather.3.cloned.1.call-done) | copy-start | bytes 6291460
  121.5 146.4 %reduce-scatter.3.cloned.1.call-start = ((), (), s32[]{:S(2)}) async-start(), calls=%async_computation.6 | async-start | bytes 10485760 | tf_op jit(solution)/shard_map/reduce_scatter | solution.py:78
  129.3 0.7 copy-start.6
  129.3 250.3 %reduce-scatter.5.cloned.1.call-start = ((), (), s32[]{:S(2)}) async-start(), calls=%async_computation.7 | async-start | bytes 147456 | tf_op jit(solution)/shard_map/reduce_scatter | solution.py:89
  318.5 64.2 %all-to-all-start.1 = ((bf16[8,128,128]{2,1,0:T(8,128)(2,1)}), bf16[8,128,128]{2,1,0:T(8,128)(2,1)}, u32[]{:S(2)}, u32[]{:S(2)}) async-start(bf16[8,128,128]{2,1,0:T(8,128)(2,1)} %slice.50), calls=%async_computation.3 | async-start | bytes 524288 | tf_op jit(solution)/shard_map/all_to_all | solution.py:90
Sparse Core Ops, SparseCore 0:
  9.6 25.5 all-gather.2
  86.3 23.4 all-gather.4
  121.7 72.7 all-reduce.2
  197.0 70.9 reduce-scatter.2
  318.6 60.9 reduce-scatter.4
